TPU v7x, 32 devices: a whole 2x2x4 slice. The times are simulated.
32 devices in a mesh: seq: 8 (over z, x), hx: 4 (over y, core).
Axes of the slice: x: 2, y: 2, z: 4, core: 2. Of those that a mesh axis runs over, the one named last changes fastest.
Arguments:
- query: bfloat16 [8192, 8192], P('seq', 'hx'), may hold values from -6 to 6
- key_in: bfloat16 [8192, 8192], P('seq', 'hx'), may hold values from -6 to 6
- value: bfloat16 [8192, 8192], P('seq', 'hx'), may hold values from -6 to 6
- head_gain: float32 [8192], P('hx'), may hold values from 0.1 to 1.9
- out_weight: bfloat16 [8192, 6144], P('hx', 'seq'), may hold values from -0.0625 to 0.0625
- residual: bfloat16 [8192, 6144], P(('seq', 'hx')), may hold values from -6 to 6
Outputs:
- mixed: bfloat16 [8192, 6144], P(('seq', 'hx'))
All inputs are finite; a program needn't handle non-finite values.
Results may differ from a plain program's by a relative error of at most 0.014.
Values may be sent and summed in bfloat16 or wider, within the bound.
A program may use at most 128 MiB of HBM per device.

v0:
```python
import jax
import jax.numpy as jnp
from jax import lax
from jax.sharding import PartitionSpec as P

DH = 128


def entering(x, axis, combine, identity):
    size, position = (lax.axis_size(axis), lax.axis_index(axis))
    everything = lax.all_gather(x.astype(jnp.bfloat16), axis)
    start = jnp.broadcast_to(jnp.asarray(identity, x.dtype), x.shape)

    def turn(k, before):
        reached = k < position
        new = combine(before, everything[k].astype(x.dtype))
        return jnp.where(reached, new, before)

    return lax.fori_loop(0, size, turn, start)


def activate(array):
    return jax.nn.silu(array.astype(jnp.float32)).astype(jnp.bfloat16)


def per_device(query, key_in, value, head_gain, out_weight, residual):
    highest = lax.Precision.HIGHEST
    tokens_here, width = query.shape
    heads = width // DH
    q_act = activate(query).reshape(tokens_here, heads, DH)
    k_act = activate(key_in).reshape(tokens_here, heads, DH)
    v_heads = value.reshape(tokens_here, heads, DH)
    blocks = min(512, tokens_here)
    count = tokens_here // blocks
    rows = jnp.arange(blocks, dtype=jnp.int32)
    lower = rows[:, None] >= rows[None, :]
    running = jnp.zeros((heads, DH, DH), jnp.float32)
    pieces = []
    for index in range(count):
        q_part = q_act[index * blocks : (index + 1) * blocks]
        k_part = k_act[index * blocks : (index + 1) * blocks]
        v_part = v_heads[index * blocks : (index + 1) * blocks]
        scores = jnp.einsum("thd,shd->hts", q_part, k_part, preferred_element_type=jnp.float32)
        scores = jnp.where(lower[None, :, :], scores, jnp.zeros_like(scores))
        inner = jnp.einsum("hts,she->the", scores, v_part.astype(jnp.float32), precision=highest)
        if index > 0:
            inner = inner + jnp.einsum(
                "thd,hde->the", q_part.astype(jnp.float32), running, precision=highest
            )
        pieces.append(inner)
        running = running + jnp.einsum(
            "thd,the->hde", k_part, v_part, preferred_element_type=jnp.float32
        )
    local_part = jnp.concatenate(pieces, axis=0)
    empty = jnp.zeros((heads, DH, DH), jnp.float32)

    def combine(earlier, later):
        return earlier + later

    prefix = entering(running, "seq", combine, empty)
    attended = local_part + jnp.einsum(
        "thd,hde->the", q_act.astype(jnp.float32), prefix, precision=highest
    )
    meansq = jnp.mean(attended * attended, axis=-1, keepdims=True)
    normed = attended * lax.rsqrt(meansq + 1e-06) * head_gain.reshape(heads, DH)
    normed = normed.astype(jnp.bfloat16).reshape(tokens_here, width)
    full_weight = lax.all_gather(out_weight, "seq", axis=1, tiled=True)
    summed = lax.psum_scatter(
        jnp.dot(normed, full_weight, preferred_element_type=jnp.float32).astype(jnp.bfloat16),
        "hx",
        scatter_dimension=0,
        tiled=True,
    ).astype(jnp.float32)
    return (summed + residual.astype(jnp.float32)).astype(jnp.bfloat16)


def solution(mesh):
    return jax.shard_map(
        per_device,
        mesh=mesh,
        in_specs=(
            P("seq", "hx"),
            P("seq", "hx"),
            P("seq", "hx"),
            P("hx"),
            P("hx", "seq"),
            P(("seq", "hx"), None),
        ),
        out_specs=P(("seq", "hx"), None),
        check_vma=False,
    )
```

profile of v0, /device:TPU:0, one launch (start us, length us, event | category | flops | bytes accessed | tf_op | source)
XLA Modules:
  0.0 733.0 jit_solution(13041921529370957699)
XLA Ops:
  6.5 6.4 copy.48
  12.9 4.1 fusion.11
  17.0 2.4 fusion.24
  20.7 1.8 fusion.23
  22.5 2.5 copy.81
  25.0 2.9 copy.80
  27.9 2.4 fusion.27
  33.9 6.4 copy.47
  40.4 4.1 fusion.7
  44.5 1.6 fusion.22
  48.6 2.4 fusion.26
  50.9 11.2 %fusion = f32[16,512,128]{2,1,0:T(8,128)} fusion(bf16[512,16,128]{0,2,1:T(8,128)(2,1)} %bitcast.44, f32[16,512,512]{2,1,0:T(8,128)S(1)} %fusion.26, pred[512,512]{1,0:T(8,128)(4,1)S(1)} %iota_compare_fusion), kind=kOutput, calls=%fused_computation.1 | convolution fusion | flops 6446645248 | bytes 23330816 | tf_op jit(solution)/shard_map/hts,she->the/dot_general | solution.py:45
  62.2 7.3 %bitcast_add_fusion = f32[512,16,128]{2,0,1:T(8,128)} fusion(f32[16,512,128]{2,1,0:T(8,128)} %fusion, f32[16,128,128]{2,1,0:T(8,128)} %copy-done.6, bf16[512,16,128]{0,2,1:T(8,128)(2,1)} %bitcast.49), kind=kOutput, calls=%fused_computation.26 | convolution fusion | flops 1611661312 | bytes 11534336 | tf_op jit(solution)/shard_map/thd,hde->the/dot_general | solution.py:47
  69.5 2.4 fusion.25
  71.9 10.0 %fusion.16 = f32[512,16,128]{2,0,1:T(8,128)} fusion(bf16[512,16,128]{0,2,1:T(8,128)(2,1)S(1)} %bitcast.41, f32[16,512,512]{2,1,0:T(8,128)S(1)} %fusion.25, pred[512,512]{1,0:T(8,128)(4,1)S(1)} %iota_compare_fusion), kind=kOutput, calls=%fused_computation.27 | convolution fusion | flops 6446645248 | bytes 23330816 | tf_op jit(solution)/shard_map/hts,she->the/dot_general | solution.py:45
  81.8 26.7 %all-gather.6.cloned.1.call-done = bf16[128,128,128]{2,1,0:T(8,128)(2,1)} async-done(((bf16[16,128,128]{2,1,0:T(8,128)(2,1)}), bf16[128,128,128]{2,1,0:T(8,128)(2,1)}) %all-gather.6.cloned.1.call-update) | async-done | bytes 4194320 | tf_op jit(solution)/shard_map/all_gather | solution.py:11
  108.6 13.2 %while.14 = (s32[]{:T(128)}, f32[16,128,128]{2,1,0:T(8,128)S(1)}, s32[]{:T(128)}, bf16[8,16,128,128]{3,2,1,0:T(8,128)(2,1)}, s32[]{:T(128)}, /*index=5*/s32[]{:T(128)}) while((s32[]{:T(128)}, f32[16,128,128]{2,1,0:T(8,128)S(1)}, s32[]{:T(128)}, bf16[8,16,128,128]{3,2,1,0:T(8,128)(2,1)}, s32[]{:T(128)}, /*index=5*/s32[]{:T(128)}) %tuple.45), condition=%wide.region_1.2_spmd.clone, body=%wide.region_0.1_spmd.clone.sunk | while | flops 1048580 | bytes 2621533 | solution.py:19
  108.6 1.6 add_select_fusion.2
  110.2 1.6 add_select_fusion.2
  111.9 1.6 add_select_fusion.2
  113.5 1.6 add_select_fusion.2
  115.1 1.7 add_select_fusion.2
  116.8 1.7 add_select_fusion.2
  118.5 1.6 add_select_fusion.2
  120.2 1.6 add_select_fusion.2
  121.8 11.0 %multiply_reduce_fusion = (f32[1024,16]{0,1:T(8,128)S(1)}, f32[1024,16,128]{2,0,1:T(8,128)}) fusion(f32[16,128,128]{2,1,0:T(8,128)S(1)} %get-tuple-element.84, bf16[1024,16,128]{0,2,1:T(8,128)(2,1)} %bitcast.39, f32[512,16,128]{2,0,1:T(8,128)} %bitcast_add_fusion, f32[512,16,128]{2,0,1:T(8,128)} %fusion.16), kind=kOutput, calls=%fused_computation.20 | convolution fusion | flops 3229597696 | bytes 22085632 | tf_op jit(solution)/shard_map/thd,hde->the/dot_general | solution.py:61
  132.8 6.9 multiply_convert_fusion
  139.7 6.4 copy.65
  146.1 442.9 %all-gather.4.cloned.1.call-done = bf16[2048,6144]{1,0:T(8,128)(2,1)} async-done(((bf16[2048,768]{1,0:T(8,128)(2,1)}), bf16[2048,6144]{1,0:T(8,128)(2,1)}) %all-gather.4.cloned.1.call-update) | async-done | bytes 25165840 | tf_op jit(solution)/shard_map/all_gather | solution.py:67
  589.1 32.9 %convolution_convert_fusion = bf16[1024,6144]{1,0:T(8,128)(2,1)} fusion(bf16[1024,2048]{0,1:T(8,128)(2,1)} %bitcast.51, bf16[2048,6144]{1,0:T(8,128)(2,1)} %all-gather.4.cloned.1.call-done), kind=kOutput, calls=%fused_computation.5 | convolution fusion | flops 25776095232 | bytes 41943040 | tf_op jit(solution)/shard_map/dot_general | solution.py:69
  622.0 99.7 %reduce-scatter.2.cloned.1.call-done = bf16[256,6144]{1,0:T(8,128)(2,1)} async-done(((bf16[1024,6144]{1,0:T(8,128)(2,1)}), bf16[256,6144]{1,0:T(8,128)(2,1)}) %reduce-scatter.2.cloned.1.call-update) | async-done | bytes 3145744 | tf_op jit(solution)/shard_map/reduce_scatter | solution.py:68
  721.7 4.7 add_convert_fusion
  (32 shorter events, 7.4 us)
Async XLA Ops:
  6.5 102.1 %all-gather.6.cloned.1.call-start = ((), (), s32[]{:S(2)}) async-start(), calls=%async_computation.3 | async-start | bytes 4718592 | tf_op jit(solution)/shard_map/all_gather | solution.py:11
  17.0 3.7 copy-start.8
  27.9 3.5 copy-start.2
  27.9 3.5 copy-start.3
  30.4 1.0 copy-start.6
  32.9 556.1 %all-gather.4.cloned.1.call-start = ((), (), s32[]{:S(2)}) async-start(), calls=%async_computation.1 | async-start | bytes 28311552 | tf_op jit(solution)/shard_map/all_gather | solution.py:67
  33.7 688.1 %reduce-scatter.2.cloned.1.call-start = ((), (), s32[]{:S(2)}) async-start(), calls=%async_computation.2 | async-start | bytes 15728640 | tf_op jit(solution)/shard_map/reduce_scatter | solution.py:68
  44.4 2.8 copy-start
  44.4 4.1 copy-start.4
  47.2 1.3 copy-start.5
  62.1 7.4 %copy-start.1 = (bf16[512,2048]{0,1:T(8,128)(2,1)S(1)}, bf16[512,2048]{0,1:T(8,128)(2,1)}, u32[]{:S(2)}) copy-start(bf16[512,2048]{0,1:T(8,128)(2,1)} %get-tuple-element.112) | copy-start | bytes 6291460
  62.1 7.4 %copy-start.7 = (bf16[512,2048]{0,1:T(8,128)(2,1)S(1)}, bf16[512,2048]{0,1:T(8,128)(2,1)}, u32[]{:S(2)}) copy-start(bf16[512,2048]{0,1:T(8,128)(2,1)} %get-tuple-element.108) | copy-start | bytes 6291460
  121.8 11.0 %copy-start.10 = (f32[2048]{0:T(1024)S(1)}, f32[2048]{0:T(1024)}, u32[]{:S(2)}) copy-start(f32[2048]{0:T(1024)} %param.11) | copy-start | bytes 24580
  622.0 99.8 %copy-start.9 = (bf16[256,6144]{1,0:T(8,128)(2,1)S(1)}, bf16[256,6144]{1,0:T(8,128)(2,1)}, u32[]{:S(2)}) copy-start(bf16[256,6144]{1,0:T(8,128)(2,1)} %param.13) | copy-start | bytes 9437188
Sparse Core Ops, SparseCore 0:
  33.0 75.4 all-gather.5
  110.1 478.8 all-gather.3
  622.1 99.5 reduce-scatter.1
where the time goes:
time: 734 us; the launch traced here: 733 us
  waiting for transfers between devices  570 us (78%)
  matrix products  81.1 us (11%)
  local copies, waits for them, and re-layouts  35.2 us (5%)
  other arithmetic  32.9 us (4%)
  between operations  13.3 us (2%)
    all_gather x1, waiting for transfers between devices, per_device(): full_weight = lax.all_gather(out_weight, 'seq', axis=1, tiled=True)  443 us
    reduce_scatter x1, waiting for transfers between devices, per_device(): lax.psum_scatter(jnp.dot(normed, full_weight, preferred_element_type=jnp....  99.7 us
    dot_general x1, matrix products, per_device(): jnp.dot(normed, full_weight, preferred_element_type=jnp.float32)  32.9 us
    all_gather x1, waiting for transfers between devices, entering(): everything = lax.all_gather(x.astype(jnp.bfloat16), axis)  26.7 us
    unnamed x26, local copies, waits for them, and re-layouts  22.9 us
    dot_general x2, matrix products, per_device(): jnp.einsum('hts,she->the', scores, v_part.astype(jnp.float32), precision=...  21.2 us
  transfers between devices with their start and end apart: 3, of which 3 were waited for; matrix products, arithmetic and copies ran while one was open for 11% of the time, Pallas kernels for 0%

commit v1 on v0

--- a/solution.py
+++ b/solution.py
@@ -1,9 +1,40 @@
+import functools
 import jax
 import jax.numpy as jnp
 from jax import lax
 from jax.sharding import PartitionSpec as P
 
 DH = 128
+
+
+def set_lay(v0, row_axis):
+    h_now = lax.axis_size(row_axis)
+    passed = lax.axis_index(row_axis)
+    out_arr, low, v_next = (h_now, passed, v0.shape[1])
+    parts_out = range(out_arr)
+    moved = map(lambda rr: (rr, (rr + 1) % out_arr), parts_out)
+    in_order = list(moved)
+    carry_out = range(out_arr)
+    o_now = map(lambda rr: (rr, (rr - 1) % out_arr), carry_out)
+    ledger = list(o_now)
+    n_now = jnp.zeros((*v0.shape[:1], out_arr * v_next, *v0.shape[2:]), v0.dtype)
+    n_now = lax.dynamic_update_slice_in_dim(n_now, v0, low * v_next, axis=1)
+    f_next = value_now = v0
+    local_next = out_arr // 2
+    for no in range(1, local_next + 1):
+        f_next = lax.ppermute(f_next, row_axis, in_order)
+        n_now = lax.dynamic_update_slice_in_dim(
+            n_now, f_next, (low - no) % out_arr * v_next, axis=1
+        )
+        if no < out_arr - local_next:
+            value_now = lax.ppermute(value_now, row_axis, ledger)
+            n_now = lax.dynamic_update_slice_in_dim(
+                n_now, value_now, (low + no) % out_arr * v_next, axis=1
+            )
+    return n_now
+
+
+_extend_pipes = functools.partial(set_lay, row_axis="seq")
 
 
 def entering(x, axis, combine, identity):
@@ -64,7 +95,7 @@
     meansq = jnp.mean(attended * attended, axis=-1, keepdims=True)
     normed = attended * lax.rsqrt(meansq + 1e-06) * head_gain.reshape(heads, DH)
     normed = normed.astype(jnp.bfloat16).reshape(tokens_here, width)
-    full_weight = lax.all_gather(out_weight, "seq", axis=1, tiled=True)
+    full_weight = _extend_pipes(out_weight)
     summed = lax.psum_scatter(
         jnp.dot(normed, full_weight, preferred_element_type=jnp.float32).astype(jnp.bfloat16),
         "hx",

time: 734 us -> 670 us (0.913)
  waiting for transfers between devices: 570 us -> 440 us
  local copies, waits for them, and re-layouts: 35.2 us -> 76.4 us
  starting transfers between devices: 0.26 us -> 20.3 us
    all_gather x1 -> x0, waiting for transfers between devices: 443 us -> none  [per_device(): full_weight = lax.all_gather(out_weight, 'seq', axis=1, tiled=True)]
    ppermute x0 -> x7, waiting for transfers between devices: none -> 342 us  [the longest x4 342 us: set_lay(): f_next = lax.ppermute(f_next, row_axis, in_order)]
    dynamic_update_slice x0 -> x8, local copies, waits for them, and re-layouts: none -> 27.3 us  [the longest x4 15.4 us: set_lay(): lax.dynamic_update_slice_in_dim(n_now, f_next, (low - no) % out_arr * v_n...]
    all_gather x1, waiting for transfers between devices: 26.7 us -> 0.01 us  [entering(): everything = lax.all_gather(x.astype(jnp.bfloat16), axis)]
    ppermute x0 -> x7, starting transfers between devices: none -> 20.3 us  [the longest x4 11.2 us: set_lay(): f_next = lax.ppermute(f_next, row_axis, in_order)]
    unnamed x26 -> x22, local copies, waits for them, and re-layouts: 22.9 us -> 29.4 us
  transfers between devices with their start and end apart: 3 -> 9, of which waited for: 3 -> 5; matrix products, arithmetic and copies ran while one was open for 11% -> 21% of each run, Pallas kernels for 0% -> 0%
where the time goes in v1:
time: 670 us; the launch traced here: 665 us
  waiting for transfers between devices  440 us (66%)
  matrix products  81.8 us (12%)
  local copies, waits for them, and re-layouts  76.4 us (11%)
  other arithmetic  32.1 us (5%)
  starting transfers between devices  20.3 us (3%)
  between operations  13.8 us (2%)
    ppermute x4, waiting for transfers between devices, set_lay(): f_next = lax.ppermute(f_next, row_axis, in_order)  342 us
    reduce_scatter x1, waiting for transfers between devices, per_device(): lax.psum_scatter(jnp.dot(normed, full_weight, preferred_element_type=jnp....  98.1 us
    dot_general x1, matrix products, per_device(): jnp.dot(normed, full_weight, preferred_element_type=jnp.float32)  32.4 us
    unnamed x22, local copies, waits for them, and re-layouts  29.4 us
    dot_general x2, matrix products, per_device(): jnp.einsum('hts,she->the', scores, v_part.astype(jnp.float32), precision=...  21.2 us
    dynamic_update_slice x4, local copies, waits for them, and re-layouts, set_lay(): lax.dynamic_update_slice_in_dim(n_now, f_next, (low - no) % out_arr * v_n...  15.4 us
  transfers between devices with their start and end apart: 9, of which 5 were waited for; matrix products, arithmetic and copies ran while one was open for 21% of the time, Pallas kernels for 0%

profile of v1, /device:TPU:0, one launch (start us, length us, event | category | flops | bytes accessed | tf_op | source)
XLA Modules:
  0.0 664.6 jit_solution(3450283047148660956)
XLA Ops:
  12.5 6.4 copy.48
  18.9 4.8 fusion.23
  26.6 3.9 copy.81
  30.5 4.1 fusion.11
  36.2 3.1 fusion.27
  41.0 6.5 copy.47
  47.4 125.3 %collective-permute-done = bf16[2048,768]{1,0:T(8,128)(2,1)} collective-permute-done((bf16[2048,768]{1,0:T(8,128)(2,1)}, bf16[2048,768]{1,0:T(8,128)(2,1)}, u32[]{:S(2)}, u32[]{:S(2)}) %collective-permute-start) | collective-permute-done | bytes 3145760 | tf_op jit(solution)/shard_map/ppermute | solution.py:25
  175.6 5.4 fusion.7
  181.1 3.9 fusion.22
  188.8 11.3 %fusion = f32[16,512,128]{2,1,0:T(8,128)} fusion(bf16[512,16,128]{0,2,1:T(8,128)(2,1)} %bitcast.42, f32[16,512,512]{2,1,0:T(8,128)S(1)} %fusion.26, pred[512,512]{1,0:T(8,128)(4,1)S(1)} %iota_compare_fusion), kind=kOutput, calls=%fused_computation.1 | convolution fusion | flops 6446645248 | bytes 23330816 | tf_op jit(solution)/shard_map/hts,she->the/dot_general | solution.py:76
  203.2 7.3 %bitcast_add_fusion = f32[512,16,128]{2,0,1:T(8,128)} fusion(f32[16,512,128]{2,1,0:T(8,128)} %fusion, f32[16,128,128]{2,1,0:T(8,128)} %copy-done.5, bf16[512,16,128]{0,2,1:T(8,128)(2,1)} %bitcast.47), kind=kOutput, calls=%fused_computation.26 | convolution fusion | flops 1611661312 | bytes 11534336 | tf_op jit(solution)/shard_map/thd,hde->the/dot_general | solution.py:78
  210.5 99.3 %collective-permute-done.2 = bf16[2048,768]{1,0:T(8,128)(2,1)} collective-permute-done((bf16[2048,768]{1,0:T(8,128)(2,1)}, bf16[2048,768]{1,0:T(8,128)(2,1)}, u32[]{:S(2)}, u32[]{:S(2)}) %collective-permute-start.2) | collective-permute-done | bytes 3145760 | tf_op jit(solution)/shard_map/ppermute | solution.py:25
  312.5 3.1 broadcast_in_dim.26
  316.0 8.3 %copy-done = bf16[2048,6144]{1,0:T(8,128)(2,1)} copy-done((bf16[2048,6144]{1,0:T(8,128)(2,1)}, bf16[2048,6144]{1,0:T(8,128)(2,1)S(1)}, u32[]{:S(2)}) %copy-start) | copy-done | bytes 25165848
  324.3 4.6 fusion.25
  328.9 9.9 %fusion.16 = f32[512,16,128]{2,0,1:T(8,128)} fusion(bf16[512,16,128]{0,2,1:T(8,128)(2,1)S(1)} %bitcast.41, f32[16,512,512]{2,1,0:T(8,128)S(1)} %fusion.25, pred[512,512]{1,0:T(8,128)(4,1)S(1)} %iota_compare_fusion), kind=kOutput, calls=%fused_computation.27 | convolution fusion | flops 6446645248 | bytes 23330816 | tf_op jit(solution)/shard_map/hts,she->the/dot_general | solution.py:76
  338.8 3.9 constant_dynamic-update-slice_fusion.6
  342.7 3.8 constant_dynamic-update-slice_fusion.5
  349.4 3.8 constant_dynamic-update-slice_fusion.4
  353.2 3.9 constant_dynamic-update-slice_fusion.3
  357.1 88.8 %collective-permute-done.4 = bf16[2048,768]{1,0:T(8,128)(2,1)} collective-permute-done((bf16[2048,768]{1,0:T(8,128)(2,1)}, bf16[2048,768]{1,0:T(8,128)(2,1)}, u32[]{:S(2)}, u32[]{:S(2)}) %collective-permute-start.4) | collective-permute-done | bytes 3145760 | tf_op jit(solution)/shard_map/ppermute | solution.py:25
  448.5 13.1 %while.14 = (s32[]{:T(128)}, f32[16,128,128]{2,1,0:T(8,128)S(1)}, s32[]{:T(128)}, bf16[8,16,128,128]{3,2,1,0:T(8,128)(2,1)}, s32[]{:T(128)}, /*index=5*/s32[]{:T(128)}) while((s32[]{:T(128)}, f32[16,128,128]{2,1,0:T(8,128)S(1)}, s32[]{:T(128)}, bf16[8,16,128,128]{3,2,1,0:T(8,128)(2,1)}, s32[]{:T(128)}, /*index=5*/s32[]{:T(128)}) %tuple.43), condition=%wide.region_1.2_spmd.clone, body=%wide.region_0.1_spmd.clone.sunk | while | flops 1048580 | bytes 2621541 | solution.py:50
  461.6 9.3 %multiply_reduce_fusion = (f32[1024,16]{0,1:T(8,128)S(1)}, f32[1024,16,128]{2,0,1:T(8,128)S(1)}) fusion(f32[16,128,128]{2,1,0:T(8,128)S(1)} %get-tuple-element.84, bf16[1024,16,128]{0,2,1:T(8,128)(2,1)} %bitcast.39, f32[512,16,128]{2,0,1:T(8,128)} %bitcast_add_fusion, f32[512,16,128]{2,0,1:T(8,128)} %fusion.16), kind=kOutput, calls=%fused_computation.20 | convolution fusion | flops 3229597696 | bytes 22085632 | tf_op jit(solution)/shard_map/thd,hde->the/dot_general | solution.py:92
  470.9 3.9 multiply_convert_fusion
  474.8 6.3 copy.65
  481.2 3.9 constant_dynamic-update-slice_fusion.2
  485.1 3.8 constant_dynamic-update-slice_fusion.1
  488.9 28.5 %collective-permute-done.6 = bf16[2048,768]{1,0:T(8,128)(2,1)} collective-permute-done((bf16[2048,768]{1,0:T(8,128)(2,1)}, bf16[2048,768]{1,0:T(8,128)(2,1)}, u32[]{:S(2)}, u32[]{:S(2)}) %collective-permute-start.6) | collective-permute-done | bytes 3145760 | tf_op jit(solution)/shard_map/ppermute | solution.py:25
  517.4 3.9 constant_dynamic-update-slice_fusion
  521.3 32.4 %convolution_convert_fusion = bf16[1024,6144]{1,0:T(8,128)(2,1)} fusion(bf16[1024,2048]{0,1:T(8,128)(2,1)S(1)} %bitcast.49, bf16[2048,6144]{1,0:T(8,128)(2,1)} %constant_dynamic-update-slice_fusion), kind=kOutput, calls=%fused_computation.5 | convolution fusion | flops 25776095232 | bytes 41943040 | tf_op jit(solution)/shard_map/dot_general | solution.py:100
  553.7 98.1 %reduce-scatter.2.cloned.1.call-done = bf16[256,6144]{1,0:T(8,128)(2,1)} async-done(((bf16[1024,6144]{1,0:T(8,128)(2,1)}), bf16[256,6144]{1,0:T(8,128)(2,1)}) %reduce-scatter.2.cloned.1.call-update) | async-done | bytes 3145744 | tf_op jit(solution)/shard_map/reduce_scatter | solution.py:99
  651.9 5.7 add_convert_fusion
  (48 shorter events, 43.6 us)
Async XLA Ops:
  6.5 442.0 %all-gather.3.cloned.1.call-start = ((), (), s32[]{:S(2)}) async-start(), calls=%async_computation.2 | async-start | bytes 4718592 | tf_op jit(solution)/shard_map/all_gather | solution.py:42
  6.5 166.1 %collective-permute-start = (bf16[2048,768]{1,0:T(8,128)(2,1)}, bf16[2048,768]{1,0:T(8,128)(2,1)}, u32[]{:S(2)}, u32[]{:S(2)}) collective-permute-start(bf16[2048,768]{1,0:T(8,128)(2,1)} %param.12), channel_id=1, source_target_pairs={{0,4},{4,8},{8,12},{12,16},{16,20},{20,24},{24,28},{28,0},{1,5},{5... | collective-permute-start | bytes 9437192 | tf_op jit(solution)/shard_map/ppermute | solution.py:25
  9.5 190.6 %collective-permute-start.1 = (bf16[2048,768]{1,0:T(8,128)(2,1)}, bf16[2048,768]{1,0:T(8,128)(2,1)}, u32[]{:S(2)}, u32[]{:S(2)}) collective-permute-start(bf16[2048,768]{1,0:T(8,128)(2,1)} %param.12), channel_id=1, source_target_pairs={{0,28},{4,0},{8,4},{12,8},{16,12},{20,16},{24,20},{28,24},{1,29},{... | collective-permute-start | bytes 9437192 | tf_op jit(solution)/shard_map/ppermute | solution.py:30
  36.2 3.1 copy-start.2
  36.2 3.1 copy-start.1
  39.3 8.1 %copy-start.5 = (f32[16,128,128]{2,1,0:T(8,128)}, f32[16,128,128]{2,1,0:T(8,128)S(1)}, u32[]{:S(2)}) copy-start(f32[16,128,128]{2,1,0:T(8,128)S(1)} %fusion.27) | copy-start | bytes 3145732
  40.9 611.0 %reduce-scatter.2.cloned.1.call-start = ((), (), s32[]{:S(2)}) async-start(), calls=%async_computation.1 | async-start | bytes 15728640 | tf_op jit(solution)/shard_map/reduce_scatter | solution.py:99
  172.7 137.2 %collective-permute-start.2 = (bf16[2048,768]{1,0:T(8,128)(2,1)}, bf16[2048,768]{1,0:T(8,128)(2,1)}, u32[]{:S(2)}, u32[]{:S(2)}) collective-permute-start(bf16[2048,768]{1,0:T(8,128)(2,1)} %collective-permute-done), channel_id=1, source_target_pairs={{0,4},{4,8},{8,12},{12,16},{16,20},{20,24},{24,28},{28,0},{1,5},{5... | collective-permute-start | bytes 9437192 | tf_op jit(solution)/shard_map/ppermute | solution.py:25
  181.1 5.3 copy-start.3
  185.1 1.4 copy-start.4
  200.1 146.4 %collective-permute-start.3 = (bf16[2048,768]{1,0:T(8,128)(2,1)}, bf16[2048,768]{1,0:T(8,128)(2,1)}, u32[]{:S(2)}, u32[]{:S(2)}) collective-permute-start(bf16[2048,768]{1,0:T(8,128)(2,1)} %collective-permute-done.1), channel_id=1, source_target_pairs={{0,28},{4,0},{8,4},{12,8},{16,12},{20,16},{24,20},{28,24},{1,29},{... | collective-permute-start | bytes 9437192 | tf_op jit(solution)/shard_map/ppermute | solution.py:30
  210.5 105.0 %copy-start.7 = (bf16[2048,768]{1,0:T(8,128)(2,1)S(1)}, bf16[2048,768]{1,0:T(8,128)(2,1)}, u32[]{:S(2)}) copy-start(bf16[2048,768]{1,0:T(8,128)(2,1)} %param.12) | copy-start | bytes 9437188
  309.8 136.0 %collective-permute-start.4 = (bf16[2048,768]{1,0:T(8,128)(2,1)}, bf16[2048,768]{1,0:T(8,128)(2,1)}, u32[]{:S(2)}, u32[]{:S(2)}) collective-permute-start(bf16[2048,768]{1,0:T(8,128)(2,1)} %collective-permute-done.2), channel_id=1, source_target_pairs={{0,4},{4,8},{8,12},{12,16},{16,20},{20,24},{24,28},{28,0},{1,5},{5... | collective-permute-start | bytes 9437192 | tf_op jit(solution)/shard_map/ppermute | solution.py:25
  316.0 8.3 %copy-start = (bf16[2048,6144]{1,0:T(8,128)(2,1)}, bf16[2048,6144]{1,0:T(8,128)(2,1)S(1)}, u32[]{:S(2)}) copy-start(bf16[2048,6144]{1,0:T(8,128)(2,1)S(1)} %constant_dynamic-update-slice_fusion.7) | copy-start | bytes 75497472
  346.5 138.6 %collective-permute-start.5 = (bf16[2048,768]{1,0:T(8,128)(2,1)}, bf16[2048,768]{1,0:T(8,128)(2,1)}, u32[]{:S(2)}, u32[]{:S(2)}) collective-permute-start(bf16[2048,768]{1,0:T(8,128)(2,1)} %collective-permute-done.3), channel_id=1, source_target_pairs={{0,28},{4,0},{8,4},{12,8},{16,12},{20,16},{24,20},{28,24},{1,29},{... | collective-permute-start | bytes 9437192 | tf_op jit(solution)/shard_map/ppermute | solution.py:30
  445.8 71.6 %collective-permute-start.6 = (bf16[2048,768]{1,0:T(8,128)(2,1)}, bf16[2048,768]{1,0:T(8,128)(2,1)}, u32[]{:S(2)}, u32[]{:S(2)}) collective-permute-start(bf16[2048,768]{1,0:T(8,128)(2,1)} %collective-permute-done.4), channel_id=1, source_target_pairs={{0,4},{4,8},{8,12},{12,16},{16,20},{20,24},{24,28},{28,0},{1,5},{5... | collective-permute-start | bytes 9437192 | tf_op jit(solution)/shard_map/ppermute | solution.py:25
  461.6 9.3 %copy-start.8 = (f32[2048]{0:T(1024)S(1)}, f32[2048]{0:T(1024)}, u32[]{:S(2)}) copy-start(f32[2048]{0:T(1024)} %param.11) | copy-start | bytes 24580
  488.9 32.4 %copy-start.6 = (bf16[1024,16,128]{0,2,1:T(8,128)(2,1)S(1)}, bf16[1024,16,128]{0,2,1:T(8,128)(2,1)}, u32[]{:S(2)}) copy-start(bf16[1024,16,128]{0,2,1:T(8,128)(2,1)} %copy.65) | copy-start | bytes 12582916
Sparse Core Ops, SparseCore 0:
  41.0 128.9 all-gather.2
  553.8 97.9 reduce-scatter.1
